TPU v7x, 32 devices: a whole 2x2x4 slice. The times are simulated.
32 devices in a mesh: site: 2 (over y), owner: 16 (over z, x, core).
Axes of the slice: x: 2, y: 2, z: 4, core: 2. Of those that a mesh axis runs over, the one named last changes fastest.
Arguments:
- green_tensor: bfloat16 [4096, 6, 1024], P(('site', 'owner')), parts along dimension 0, may hold values from -6 to 6
- mechanism: float32 [2, 6, 2048], P(None, None, 'owner'), may hold values from -2.5 to 2.5
- point_owner: int32 [16, 128, 1], P('owner'), may hold values from 0 to 15; in each aligned block of 128 rows (0 to 127, 128 to 255, ..., all dimensions but the last counted through in order) at most 16 rows name the same one
- point_row: int32 [16, 128], P('owner'), may hold values from 0 to 127
- onset_step: int32 [16, 128], P('owner'), may hold values from 0 to 511
- slip_amount: float32 [16, 128], P('owner'), may hold values from 0.01 to 0.1
- point_count: int32 [16], P('owner'), may hold values from 12 to 128
- rake_angle: float32 [16], P('owner'), may hold values from -3.140625 to 3.140625
- slip_rate: float32 [16, 64], P('owner'), may hold values from 0.02 to 0.2
Outputs:
- seismogram: float32 [32, 1024], P(('site', 'owner')), parts along dimension 0
There are 2 independent parts, one for each index of `site`. A program takes and returns all parts, laid end to end along the dimension named above; an argument that names none is the same for every part. Nothing has to cross between parts.
Inputs may be any that keep to these rules, and one draw needn't show every extreme that they name: `point_owner`: among the 128 entries of one device's variations, at most 16 name the same owner, a bound that some block reaches of them.
All inputs are finite; a program needn't handle non-finite values.
Results may differ from a plain program's by a relative error of at most 0.0029.
Values may be sent and summed in bfloat16 or wider, within the bound.
No kernel may reach another device: no remote copies, remote signals or barrier semaphores. Data moves between devices by JAX's collectives and lax.ppermute only.
A program may use at most 64 MiB of HBM per device.

v0:
```python
import jax
import jax.numpy as jnp
from jax import lax
from jax.sharding import PartitionSpec as P


def delay_rows(signal, steps):
    length = signal.shape[-1]
    step_grid = steps[..., None]
    result = signal
    for bit in range((length - 1).bit_length()):
        amount = 1 << bit
        pad_shape = signal.shape[:-1] + (amount,)
        moved = jnp.concatenate(
            [jnp.zeros(pad_shape, signal.dtype), result[..., : length - amount]], axis=-1
        )
        taken = step_grid >> bit & 1 == 1
        result = jnp.where(taken, moved, result)
    return result


def smooth(signal, kernel):
    taps = kernel.shape[1]
    filtered = lax.conv_general_dilated(
        signal[None],
        kernel[:, None, ::-1],
        (1,),
        ((taps - 1, 0),),
        dimension_numbers=("NCH", "OIH", "NCH"),
        feature_group_count=signal.shape[0],
        precision=lax.Precision.HIGHEST,
    )
    return filtered[0]


def project(green_block, mech_block):
    return jnp.einsum(
        "kcp,pct->pkt", mech_block, green_block.astype(jnp.float32), precision=lax.Precision.HIGHEST
    ).astype(jnp.bfloat16)


def coefficients(slip_amount, point_count, rake_angle):
    length = slip_amount.shape[1]
    alive_mask = jnp.arange(length, dtype=jnp.int32)[None, :] < point_count[:, None]
    weight = jnp.where(alive_mask, slip_amount, jnp.zeros_like(slip_amount))
    return jnp.stack(
        [jnp.cos(rake_angle)[:, None] * weight, jnp.sin(rake_angle)[:, None] * weight], axis=2
    )


def local(
    green_tensor,
    mechanism,
    point_owner,
    point_row,
    onset_step,
    slip_amount,
    point_count,
    rake_angle,
    slip_rate,
):
    owners = lax.axis_size("owner")
    variations, length = point_row.shape
    entries = variations * length
    capacity = 2 * entries // owners
    traces = project(green_tensor, mechanism)
    coefficient = coefficients(slip_amount, point_count, rake_angle)
    owner_flat = point_owner.reshape(entries)
    one_hot = (owner_flat[:, None] == jnp.arange(owners, dtype=jnp.int32)[None, :]).astype(
        jnp.int32
    )
    owner_rank = jnp.sum((jnp.cumsum(one_hot, axis=0) - one_hot) * one_hot, axis=1)
    slot_index = owner_flat * capacity + owner_rank
    rows_flat = point_row.reshape(entries)
    delay_flat = onset_step.reshape(entries)
    asked_rows = (
        jnp.zeros((owners * capacity,), jnp.int32)
        .at[slot_index]
        .set(rows_flat)
        .reshape(owners, capacity)
    )
    received = lax.all_to_all(
        traces[lax.all_to_all(asked_rows, "owner", split_axis=0, concat_axis=0, tiled=True)],
        "owner",
        split_axis=0,
        concat_axis=0,
        tiled=True,
    )
    own_traces = received.reshape(owners * capacity, 2, -1)[slot_index]
    coef_flat = coefficient.reshape(entries, 2)
    combined = (
        own_traces[:, 0, :].astype(jnp.float32) * coef_flat[:, 0:1]
        + own_traces[:, 1, :].astype(jnp.float32) * coef_flat[:, 1:2]
    )
    shifted = delay_rows(combined, delay_flat).reshape(variations, length, -1)
    summed = jnp.sum(shifted, axis=1)
    return smooth(summed, slip_rate)


def solution(mesh):
    in_specs = (
        P(("site", "owner"), None, None),
        P(None, None, "owner"),
        P("owner", None, None),
        P("owner", None),
        P("owner", None),
        P("owner", None),
        P("owner"),
        P("owner"),
        P("owner", None),
    )
    out_specs = P(("site", "owner"), None)
    return jax.shard_map(local, mesh=mesh, in_specs=in_specs, out_specs=out_specs, check_vma=False)
```

profile of v0, /device:TPU:0, one launch (start us, length us, event | category | flops | bytes accessed | tf_op | source)
XLA Modules:
  0.0 113.2 jit_solution(7773489332718156675)
XLA Ops:
  0.0 0.0 copy-start
  0.0 0.9 fusion.7
  0.9 0.2 reduce_window_sum.11
  1.0 0.8 select_reduce_fusion.1
  1.9 0.7 fusion.8
  2.5 1.1 scatter_custom_fusion
  3.6 0.7 all_to_all.11
  4.3 7.4 %all-to-all-start = ((s32[16,1,16]{2,1,0:T(1,128)}), s32[16,1,16]{2,1,0:T(1,128)S(1)}, u32[]{:S(2)}, u32[]{:S(2)}) async-start(s32[16,1,16]{2,1,0:T(1,128)} %all_to_all.11), calls=%async_computation | async-start | bytes 16384 | tf_op jit(solution)/shard_map/all_to_all | solution.py:83
  11.7 0.8 copy.21
  12.6 0.0 copy-done
  12.6 2.4 %fusion.2 = bf16[128,2,1024]{2,1,0:T(2,128)(2,1)S(1)} fusion(f32[2,6,128]{1,0,2:T(2,128)S(1)} %copy.21, bf16[128,6,1024]{2,0,1:T(8,128)(2,1)S(1)} %copy-done), kind=kOutput, calls=%fused_computation.5 | convolution fusion | flops 19136512 | bytes 2103296 | tf_op jit(solution)/shard_map/kcp,pct->pkt/dot_general | solution.py:37
  15.0 3.2 %all-to-all-done = s32[16,1,16]{2,1,0:T(1,128)S(1)} async-done(((s32[16,1,16]{2,1,0:T(1,128)}), s32[16,1,16]{2,1,0:T(1,128)S(1)}, u32[]{:S(2)}, u32[]{:S(2)}) %all-to-all-start) | async-done | bytes 1056 | tf_op jit(solution)/shard_map/all_to_all | solution.py:83
  18.2 0.1 reshape.286
  18.3 3.7 %gather_fusion = bf16[256,2,1024]{2,1,0:T(2,128)(2,1)} fusion(bf16[128,2,1024]{2,1,0:T(2,128)(2,1)S(1)} %fusion.2, s32[1024]{0:T(1024)S(1)} %pad_clamp_fusion.1), kind=kCustom, calls=%fused_computation | custom fusion | bytes 2098176 | tf_op jit(solution)/shard_map/gather | solution.py:83
  21.9 0.0 copy-start.3
  21.9 0.0 copy-start.1
  21.9 0.0 copy-start.2
  21.9 4.0 %all-to-all-start.1 = ((bf16[16,16,2,1024]{3,2,1,0:T(2,128)(2,1)}), bf16[16,16,2,1024]{3,2,1,0:T(2,128)(2,1)S(1)}, u32[]{:S(2)}, u32[]{:S(2)}) async-start(bf16[16,16,2,1024]{3,2,1,0:T(2,128)(2,1)} %bitcast.16), calls=%async_computation.1 | async-start | bytes 2097152 | tf_op jit(solution)/shard_map/all_to_all | solution.py:82
  27.4 0.0 copy-done.3
  27.4 0.1 rev.3
  27.5 0.1 copy.25
  27.6 0.0 copy-done.1
  27.6 0.0 copy-done.2
  27.6 20.9 %all-to-all-done.1 = bf16[16,16,2,1024]{3,2,1,0:T(2,128)(2,1)S(1)} async-done(((bf16[16,16,2,1024]{3,2,1,0:T(2,128)(2,1)}), bf16[16,16,2,1024]{3,2,1,0:T(2,128)(2,1)S(1)}, u32[]{:S(2)}, u32[]{:S(2)}) %all-to-all-start.1) | async-done | bytes 1048608 | tf_op jit(solution)/shard_map/all_to_all | solution.py:82
  48.6 1.6 %gather_fusion.1 = bf16[128,2,1024]{2,1,0:T(2,128)(2,1)S(1)} fusion(bf16[256,2,1024]{2,1,0:T(2,128)(2,1)S(1)} %bitcast.83, s32[1024]{0:T(1024)S(1)} %pad_clamp_fusion), kind=kCustom, calls=%fused_computation.1 | custom fusion | bytes 1049088 | tf_op jit(solution)/shard_map/gather | solution.py:89
  50.2 0.7 fusion.11
  50.9 0.2 fusion.5
  51.1 0.2 pad_select_fusion.8
  51.4 0.2 pad_select_fusion.7
  51.6 0.2 pad_select_fusion.6
  51.8 0.2 pad_select_fusion.5
  52.0 0.2 pad_select_fusion.4
  52.3 0.2 pad_select_fusion.3
  52.5 0.2 pad_select_fusion.2
  52.7 0.1 pad_select_fusion.1
  52.9 0.0 copy-start.4
  52.9 0.1 pad_select_fusion
  53.1 0.1 select_reduce_fusion
  53.2 0.1 pad_reduce_fusion
  53.3 0.1 reshape.270
  53.4 0.1 select_maximum_fusion
  53.5 0.1 copy.24
  53.6 0.2 copy-done.4
  53.8 58.3 %convolution_select_fusion = f32[8,136,1]{2,0,1:T(8,128)S(1)} fusion(pred[8,136,1]{2,0,1:T(8,128)(4,1)S(1)} %copy-done.4, f32[1,1,64]{1,0,2:T(1,128)S(1)} %copy.25, f32[1,1,8,199]{2,0,3,1:T(1,128)S(1)} %copy.24), kind=kOutput, calls=%fused_computation.6 | convolution fusion | flops 836672 | bytes 12064 | tf_op jit(solution)/shard_map/conv_general_dilated | solution.py:24
  112.2 0.3 copy.26
  112.5 0.1 reshape.274
  112.6 0.6 slice_bitcast_fusion
  (11 shorter events, 0.1 us)
Async XLA Ops:
  0.0 12.6 %copy-start = (bf16[128,6,1024]{2,0,1:T(8,128)(2,1)S(1)}, bf16[128,6,1024]{2,0,1:T(8,128)(2,1)}, u32[]{:S(2)}) copy-start(bf16[128,6,1024]{2,0,1:T(8,128)(2,1)} %param.9) | copy-start | bytes 4718596
  4.3 13.8 %all-to-all-start = ((s32[16,1,16]{2,1,0:T(1,128)}), s32[16,1,16]{2,1,0:T(1,128)S(1)}, u32[]{:S(2)}, u32[]{:S(2)}) async-start(s32[16,1,16]{2,1,0:T(1,128)} %all_to_all.11), calls=%async_computation | async-start | bytes 16384 | tf_op jit(solution)/shard_map/all_to_all | solution.py:83
  21.9 5.4 %copy-start.3 = (f32[1,64]{1,0:T(1,128)S(1)}, f32[1,64]{1,0:T(1,128)}, u32[]{:S(2)}) copy-start(f32[1,64]{1,0:T(1,128)} %param.17) | copy-start | bytes 772
  21.9 5.6 %copy-start.1 = (f32[1,128]{1,0:T(1,128)S(1)}, f32[1,128]{1,0:T(1,128)}, u32[]{:S(2)}) copy-start(f32[1,128]{1,0:T(1,128)} %param.14) | copy-start | bytes 1540
  21.9 5.7 %copy-start.2 = (s32[1,128]{1,0:T(1,128)S(1)}, s32[1,128]{1,0:T(1,128)}, u32[]{:S(2)}) copy-start(s32[1,128]{1,0:T(1,128)} %param.13) | copy-start | bytes 1540
  21.9 26.6 %all-to-all-start.1 = ((bf16[16,16,2,1024]{3,2,1,0:T(2,128)(2,1)}), bf16[16,16,2,1024]{3,2,1,0:T(2,128)(2,1)S(1)}, u32[]{:S(2)}, u32[]{:S(2)}) async-start(bf16[16,16,2,1024]{3,2,1,0:T(2,128)(2,1)} %bitcast.16), calls=%async_computation.1 | async-start | bytes 2097152 | tf_op jit(solution)/shard_map/all_to_all | solution.py:82
  52.9 0.9 copy-start.4
where the time goes:
time: 115 us; the launch traced here: 113 us
  matrix products  60.7 us (53%)
  waiting for transfers between devices  24.1 us (21%)
  starting transfers between devices  11.3 us (10%)
  local copies, waits for them, and re-layouts  9.87 us (9%)
  other arithmetic  5.42 us (5%)
  between operations  1.72 us (1%)
    conv_general_dilated x1, matrix products, smooth(): lax.conv_general_dilated(signal[None], kernel[:, None, ::-1], (1,), ((tap...  58.3 us
    all_to_all x1, waiting for transfers between devices, local(): lax.all_to_all(traces[lax.all_to_all(asked_rows, 'owner', split_axis=0, c...  20.9 us
    all_to_all x1, starting transfers between devices, local(): lax.all_to_all(asked_rows, 'owner', split_axis=0, concat_axis=0, tiled=True)  7.39 us
    all_to_all x1, starting transfers between devices, local(): lax.all_to_all(traces[lax.all_to_all(asked_rows, 'owner', split_axis=0, c...  3.96 us
    gather x1, local copies, waits for them, and re-layouts, local(): traces[lax.all_to_all(asked_rows, 'owner', split_axis=0, concat_axis=0, t...  3.67 us
    all_to_all x1, waiting for transfers between devices, local(): lax.all_to_all(asked_rows, 'owner', split_axis=0, concat_axis=0, tiled=True)  3.21 us
    dot_general x1, matrix products, project(): jnp.einsum('kcp,pct->pkt', mech_block, green_block.astype(jnp.float32), p...  2.37 us
  transfers between devices with their start and end apart: 2, of which 2 were waited for; matrix products, arithmetic and copies ran while one was open for 3% of the time, Pallas kernels for 0%

commit v1 on v0

v1 whole, which is shorter than its diff:
```python
import functools

import jax
import jax.numpy as jnp
from jax import lax
from jax.experimental import pallas as pl
from jax.experimental.pallas import tpu as pltpu
from jax.sharding import PartitionSpec as P

LANES = 128
FIELDS = 4
VMEM = pl.BlockSpec(memory_space=pltpu.VMEM)
SMEM = pl.BlockSpec(memory_space=pltpu.SMEM)


def route_kernel(capacity, rows, count_ref, rake_ref, owner_ref, row_ref, onset_ref, slip_ref, out_ref):
    owners = out_ref.shape[0]
    length = row_ref.shape[1]
    lane = lax.broadcasted_iota(jnp.int32, (1, length), 1)
    alive = lane < count_ref[0]
    onset = onset_ref[...]
    whole = onset // LANES
    base = row_ref[...] * (4 * rows) + rows - whole
    rake = jnp.full((1, length), rake_ref[0], jnp.float32)
    weight = jnp.where(alive, slip_ref[...], 0.0)
    fields = (
        base.astype(jnp.float32),
        (onset - whole * LANES).astype(jnp.float32),
        jnp.cos(rake) * weight,
        jnp.sin(rake) * weight,
    )
    owner_index = lax.broadcasted_iota(jnp.int32, (owners, length), 0)
    hot = ((owner_index == owner_ref[...]) & alive).astype(jnp.float32)
    earlier = lax.broadcasted_iota(jnp.int32, (length, length), 0) < lax.broadcasted_iota(
        jnp.int32, (length, length), 1
    )
    before = jnp.dot(hot, earlier.astype(jnp.float32), preferred_element_type=jnp.float32)
    rank = jnp.sum(hot * before, axis=0, keepdims=True).astype(jnp.int32)
    place = lax.broadcasted_iota(jnp.int32, (LANES, length), 0)
    spread = jnp.zeros((LANES, length), jnp.float32)
    for number, field in enumerate(fields):
        spread = jnp.where(place == rank + number * capacity, field, spread)
    out_ref[...] = lax.dot_general(
        hot,
        spread,
        (((1,), (1,)), ((), ())),
        precision=lax.Precision.HIGHEST,
        preferred_element_type=jnp.float32,
    )


def project_kernel(rows, mech_ref, green_ref, out_ref, flat_ref, column_ref):
    parts, points, _ = green_ref.shape
    flat_ref[...] = jnp.zeros_like(flat_ref)
    for part in range(parts):
        for kind in range(2):
            flat_ref[2 * part + kind : 2 * part + kind + 1, :] = mech_ref[part, kind : kind + 1, :]
    column_ref[...] = flat_ref[...].T
    group = 16
    blank = jnp.zeros((rows, LANES), jnp.float32)

    def clear(number, carry):
        out_ref[pl.ds(pl.multiple_of(number * 2 * rows, rows), rows), :] = blank
        return carry

    lax.fori_loop(0, 2 * points, clear, 0, unroll=8)

    def one(number, carry):
        first = pl.multiple_of(number * group, group)
        scale = [
            jnp.broadcast_to(column_ref[pl.ds(first, group), i : i + 1], (group, LANES))
            for i in range(2 * parts)
        ]
        for step in range(rows):
            total = [jnp.zeros((group, LANES), jnp.float32)] * 2
            for part in range(parts):
                block = green_ref[part, pl.ds(first, group), step * LANES : (step + 1) * LANES].astype(
                    jnp.float32
                )
                total = [total[kind] + scale[2 * part + kind] * block for kind in range(2)]
            for kind in range(2):
                kept = total[kind].astype(jnp.bfloat16).astype(jnp.float32)
                for half in range(group // 8):
                    start = (first + half * 8) * (4 * rows) + kind * 2 * rows + rows + step
                    out_ref[pl.ds(start, 8, stride=4 * rows), :] = kept[half * 8 : half * 8 + 8]
        return carry

    lax.fori_loop(0, points // group, one, 0)


def gather_kernel(capacity, rows, table_ref, trace_ref, out_ref):
    lane = lax.broadcasted_iota(jnp.int32, (rows, LANES), 1)

    def one(number, carry):
        total = jnp.zeros((rows, LANES), jnp.float32)
        for slot in range(capacity):
            place = number * LANES + slot
            base = table_ref[place].astype(jnp.int32)
            shift = table_ref[place + capacity].astype(jnp.int32)
            first = table_ref[place + 2 * capacity]
            second = table_ref[place + 3 * capacity]
            base = jnp.maximum(base, 1)
            stays = lane < LANES - shift
            one_kind = jnp.where(
                stays, trace_ref[pl.ds(base, rows), :], trace_ref[pl.ds(base - 1, rows), :]
            )
            base = base + 2 * rows
            other_kind = jnp.where(
                stays, trace_ref[pl.ds(base, rows), :], trace_ref[pl.ds(base - 1, rows), :]
            )
            total = total + pltpu.roll(one_kind * first + other_kind * second, shift, 1)
        out_ref[number] = total
        return carry

    lax.fori_loop(0, out_ref.shape[0], one, 0)


def smooth_kernel(taps, rate_ref, part_ref, out_ref):
    signal = jnp.sum(part_ref[...], axis=0)
    rows = signal.shape[0]
    row = lax.broadcasted_iota(jnp.int32, (rows, LANES), 0)
    lane = lax.broadcasted_iota(jnp.int32, (rows, LANES), 1)
    previous = jnp.where(row == 0, 0.0, pltpu.roll(signal, 1, 0))
    total = [signal * rate_ref[0]] + [jnp.zeros_like(signal)] * 3
    for tap in range(1, taps):
        moved = pltpu.roll(jnp.where(lane < LANES - tap, signal, previous), tap, 1)
        total[tap % 4] = total[tap % 4] + moved * rate_ref[tap]
    out_ref[...] = (total[0] + total[1]) + (total[2] + total[3])


def local(
    green_tensor,
    mechanism,
    point_owner,
    point_row,
    onset_step,
    slip_amount,
    point_count,
    rake_angle,
    slip_rate,
):
    owners = lax.axis_size("owner")
    variations, length = point_row.shape
    points, parts, steps = green_tensor.shape
    taps = slip_rate.shape[1]
    rows = steps // LANES
    capacity = 2 * length // owners
    assert variations == 1 and capacity * FIELDS <= LANES
    table = pl.pallas_call(
        functools.partial(route_kernel, capacity, rows),
        out_shape=jax.ShapeDtypeStruct((owners, LANES), jnp.float32),
        in_specs=[SMEM, SMEM, VMEM, VMEM, VMEM, VMEM],
        out_specs=VMEM,
        name="route",
    )(point_count, rake_angle, point_owner.reshape(1, length), point_row, onset_step, slip_amount)
    table = lax.all_to_all(
        table.reshape(owners, 1, LANES), "owner", split_axis=0, concat_axis=0, tiled=True
    )
    traces = pl.pallas_call(
        functools.partial(project_kernel, rows),
        out_shape=jax.ShapeDtypeStruct((points * 4 * rows, LANES), jnp.float32),
        in_specs=[VMEM, VMEM],
        out_specs=VMEM,
        scratch_shapes=[pltpu.VMEM((LANES, points), jnp.float32), pltpu.VMEM((points, LANES), jnp.float32)],
        name="project",
    )(jnp.transpose(mechanism, (1, 0, 2)), jnp.transpose(green_tensor, (1, 0, 2)))
    partial = pl.pallas_call(
        functools.partial(gather_kernel, capacity, rows),
        out_shape=jax.ShapeDtypeStruct((owners, rows, LANES), jnp.float32),
        in_specs=[SMEM, VMEM],
        out_specs=VMEM,
        name="gather",
    )(table.reshape(owners * LANES), traces)
    partial = lax.all_to_all(partial, "owner", split_axis=0, concat_axis=0, tiled=True)
    result = pl.pallas_call(
        functools.partial(smooth_kernel, taps),
        out_shape=jax.ShapeDtypeStruct((rows, LANES), jnp.float32),
        in_specs=[SMEM, VMEM],
        out_specs=VMEM,
        name="smooth",
    )(slip_rate.reshape(taps), partial)
    return result.reshape(1, steps)


def solution(mesh):
    in_specs = (
        P(("site", "owner"), None, None),
        P(None, None, "owner"),
        P("owner", None, None),
        P("owner", None),
        P("owner", None),
        P("owner", None),
        P("owner"),
        P("owner"),
        P("owner", None),
    )
    out_specs = P(("site", "owner"), None)
    return jax.shard_map(local, mesh=mesh, in_specs=in_specs, out_specs=out_specs, check_vma=False)
```

time: 115 us -> 35.7 us (0.31); the launches traced: 113 us -> 35.4 us
  matrix products: 60.7 us -> 0 us
  waiting for transfers between devices: 24.1 us -> 1.45 us
  Pallas kernels: 0 us -> 13.1 us
  blocking collectives: 0 us -> 11.6 us
  local copies, waits for them, and re-layouts: 9.87 us -> 0.59 us
  other arithmetic: 5.42 us -> 0 us
  starting transfers between devices: 11.3 us -> 7.39 us
    conv_general_dilated x1 -> x0, matrix products: 58.3 us -> none  [smooth(): lax.conv_general_dilated(signal[None], kernel[:, None, ::-1], (1,), ((tap...]
    all_to_all x2 -> x1, waiting for transfers between devices: 24.1 us -> 1.45 us  [local(): lax.all_to_all(table.reshape(owners, 1, LANES), 'owner', split_axis=0, co...]
    pallas_call x0 -> x4, Pallas kernels: none -> 13.1 us  [the longest x1 4.98 us: local(): pl.pallas_call(functools.partial(project_kernel, rows), out_shape=jax.Sha...]
    all_to_all x0 -> x1, blocking collectives: none -> 11.6 us  [local(): lax.all_to_all(partial, 'owner', split_axis=0, concat_axis=0, tiled=True)]
    gather x2 -> x0, local copies, waits for them, and re-layouts: 5.3 us -> none  [the longest x1 3.67 us: local(): traces[lax.all_to_all(asked_rows, 'owner', split_axis=0, concat_axis=0, t...]
    all_to_all x2 -> x1, starting transfers between devices: 11.3 us -> 7.39 us  [local(): lax.all_to_all(table.reshape(owners, 1, LANES), 'owner', split_axis=0, co...]
    select_n x11 -> x0, other arithmetic: 2.42 us -> none  [the longest x9 1.74 us: delay_rows(): result = jnp.where(taken, moved, result)]
    dot_general x1 -> x0, matrix products: 2.37 us -> none  [project(): jnp.einsum('kcp,pct->pkt', mech_block, green_block.astype(jnp.float32), p...]
  transfers between devices with their start and end apart: 2 -> 1, of which waited for: 2 -> 1; matrix products, arithmetic and copies ran while one was open for 3% -> 0% of each run, Pallas kernels for 0% -> 14%
where the time goes in v1:
time: 35.7 us; the launch traced here: 35.4 us
  Pallas kernels  13.1 us (37%)
  blocking collectives  11.6 us (32%)
  starting transfers between devices  7.39 us (21%)
  waiting for transfers between devices  1.45 us (4%)
  between operations  1.31 us (4%)
  local copies, waits for them, and re-layouts  0.59 us (2%)
    all_to_all x1, blocking collectives, local(): lax.all_to_all(partial, 'owner', split_axis=0, concat_axis=0, tiled=True)  11.6 us
    all_to_all x1, starting transfers between devices, local(): lax.all_to_all(table.reshape(owners, 1, LANES), 'owner', split_axis=0, co...  7.39 us
    pallas_call x1, Pallas kernels, local(): pl.pallas_call(functools.partial(project_kernel, rows), out_shape=jax.Sha...  4.98 us
    pallas_call x1, Pallas kernels, local(): pl.pallas_call(functools.partial(gather_kernel, capacity, rows), out_shap...  4.83 us
    pallas_call x1, Pallas kernels, local(): pl.pallas_call(functools.partial(route_kernel, capacity, rows), out_shape...  1.66 us
    pallas_call x1, Pallas kernels, local(): pl.pallas_call(functools.partial(smooth_kernel, taps), out_shape=jax.Shap...  1.6 us
    all_to_all x1, waiting for transfers between devices, local(): lax.all_to_all(table.reshape(owners, 1, LANES), 'owner', split_axis=0, co...  1.45 us
  transfers between devices with their start and end apart: 1, of which 1 were waited for; matrix products, arithmetic and copies ran while one was open for 0% of the time, Pallas kernels for 14%

profile of v1, /device:TPU:0, one launch (start us, length us, event | category | flops | bytes accessed | tf_op | source)
XLA Modules:
  0.0 35.4 jit_solution(5723843153228052075)
XLA Ops:
  1.3 1.7 %route.1 = f32[16,128]{1,0:T(8,128)} custom-call(s32[1]{0:T(128)S(6)} %copy.11.count_ref, f32[1]{0:T(128)S(6)} %copy.12.rake_ref, s32[1,128]{1,0:T(1,128)} %bitcast.14, s32[1,128]{1,0:T(1,128)} %row_ref.1, s32[1,128]{1,0:T(1,128)} %onset_ref.1, f32[1,128]{1,0:T(1,128)} %slip_ref.1), custom_call_target="tpu_custom_call" | custom-call | tf_op jit(solution)/shard_map/route/pallas_call | solution.py:149
  3.0 7.4 %all-to-all-start = ((f32[16,1,128]{2,1,0:T(1,128)}), f32[16,1,128]{2,1,0:T(1,128)S(1)}, u32[]{:S(2)}, u32[]{:S(2)}) async-start(f32[16,1,128]{2,1,0:T(1,128)} %bitcast.11), calls=%async_computation | async-start | bytes 16384 | tf_op jit(solution)/shard_map/all_to_all | solution.py:156
  10.3 5.0 %project.1.trace_ref = f32[4096,128]{1,0:T(8,128)} custom-call(f32[6,2,128]{2,1,0:T(2,128)} %bitcast.12, bf16[6,128,1024]{2,1,0:T(8,128)(2,1)} %bitcast.9), custom_call_target="tpu_custom_call" | custom-call | tf_op jit(solution)/shard_map/project/pallas_call | solution.py:159
  15.3 1.5 %all-to-all-done = f32[16,1,128]{2,1,0:T(1,128)S(1)} async-done(((f32[16,1,128]{2,1,0:T(1,128)}), f32[16,1,128]{2,1,0:T(1,128)S(1)}, u32[]{:S(2)}, u32[]{:S(2)}) %all-to-all-start) | async-done | bytes 8224 | tf_op jit(solution)/shard_map/all_to_all | solution.py:156
  16.8 0.0 copy-start
  16.8 0.6 %copy-done = f32[16,1,128]{2,1,0:T(1,128)} copy-done((f32[16,1,128]{2,1,0:T(1,128)}, f32[16,1,128]{2,1,0:T(1,128)S(1)}, u32[]{:S(2)}) %copy-start) | copy-done | bytes 8216
  17.4 4.8 %gather.1 = f32[16,8,128]{2,1,0:T(8,128)} custom-call(f32[2048]{0:T(1024)} %bitcast.10, f32[4096,128]{1,0:T(8,128)} %project.1.trace_ref), custom_call_target="tpu_custom_call" | custom-call | tf_op jit(solution)/shard_map/gather/pallas_call | solution.py:167
  22.2 11.6 %all_to_all.10.part_ref = f32[16,8,128]{2,1,0:T(8,128)} all-to-all(f32[16,8,128]{2,1,0:T(8,128)} %gather.1), channel_id=1, replica_groups=mesh['site'=2,'owner'=16] {'owner'}, dimensions={0} | all-to-all | bytes 131072 | tf_op jit(solution)/shard_map/all_to_all | solution.py:174
  33.8 1.6 %smooth.1 = f32[8,128]{1,0:T(8,128)} custom-call(f32[64]{0:T(128)} %bitcast.13, f32[16,8,128]{2,1,0:T(8,128)} %all_to_all.10.part_ref), custom_call_target="tpu_custom_call" | custom-call | tf_op jit(solution)/shard_map/smooth/pallas_call | solution.py:175
Async XLA Ops:
  3.0 13.8 %all-to-all-start = ((f32[16,1,128]{2,1,0:T(1,128)}), f32[16,1,128]{2,1,0:T(1,128)S(1)}, u32[]{:S(2)}, u32[]{:S(2)}) async-start(f32[16,1,128]{2,1,0:T(1,128)} %bitcast.11), calls=%async_computation | async-start | bytes 16384 | tf_op jit(solution)/shard_map/all_to_all | solution.py:156
  16.8 0.6 %copy-start = (f32[16,1,128]{2,1,0:T(1,128)}, f32[16,1,128]{2,1,0:T(1,128)S(1)}, u32[]{:S(2)}) copy-start(f32[16,1,128]{2,1,0:T(1,128)S(1)} %all-to-all-done) | copy-start | bytes 24580

commit v2 on v1

v2 whole, which is shorter than its diff:
```python
import functools

import jax
import jax.numpy as jnp
from jax import lax
from jax.experimental import pallas as pl
from jax.experimental.pallas import tpu as pltpu
from jax.sharding import PartitionSpec as P

LANES = 128
FIELDS = 4
ANY = pl.BlockSpec(memory_space=pltpu.HBM)
VMEM = pl.BlockSpec(memory_space=pltpu.VMEM)
SMALL = pltpu.CompilerParams(vmem_limit_bytes=16 << 20)


def in_hbm(array):
    return pltpu.with_memory_space_constraint(array, pltpu.HBM)


def in_vmem(array):
    return pltpu.with_memory_space_constraint(array, pltpu.VMEM)


def fetch(sources, targets, arrived):
    copies = [
        pltpu.make_async_copy(source, target, arrived.at[number])
        for number, (source, target) in enumerate(zip(sources, targets))
    ]
    for copy in copies:
        copy.start()
    for copy in copies:
        copy.wait()


def route_kernel(capacity, rows, *refs):
    sources, out_ref, targets, arrived = refs[:6], refs[6], refs[7:13], refs[13]
    fetch(sources, targets, arrived)
    owner_ref, row_ref, onset_ref, slip_ref, count_ref, rake_ref = targets
    owners = out_ref.shape[0]
    length = row_ref.shape[1]
    lane = lax.broadcasted_iota(jnp.int32, (1, length), 1)
    alive = lane < count_ref[0]
    onset = onset_ref[...]
    whole = onset // LANES
    base = row_ref[...] * (4 * rows) + (rows - 1) - whole
    rake = jnp.full((1, length), rake_ref[0], jnp.float32)
    weight = jnp.where(alive, slip_ref[...], 0.0)
    fields = (
        base.astype(jnp.float32),
        (onset - whole * LANES).astype(jnp.float32),
        jnp.cos(rake) * weight,
        jnp.sin(rake) * weight,
    )
    owner_index = lax.broadcasted_iota(jnp.int32, (owners, length), 0)
    hot = ((owner_index == owner_ref[...]) & alive).astype(jnp.float32)
    earlier = lax.broadcasted_iota(jnp.int32, (length, length), 0) < lax.broadcasted_iota(
        jnp.int32, (length, length), 1
    )
    before = jnp.dot(hot, earlier.astype(jnp.float32), preferred_element_type=jnp.float32)
    rank = jnp.sum(hot * before, axis=0, keepdims=True).astype(jnp.int32)
    place = lax.broadcasted_iota(jnp.int32, (LANES, length), 0)
    spread = jnp.zeros((LANES, length), jnp.float32)
    for number, field in enumerate(fields):
        spread = jnp.where(place == rank + number * capacity, field, spread)
    out_ref[...] = lax.dot_general(
        hot,
        spread,
        (((1,), (1,)), ((), ())),
        precision=lax.Precision.HIGHEST,
        preferred_element_type=jnp.float32,
    )


def project_kernel(
    rows, group, chunk, mech_ref, rate_ref, green_ref, out_ref, rates_ref,
    mech_here, rate_here, green_here, flat_ref, column_ref, arrived, landed,
):
    parts, points, _ = green_ref.shape
    small = [
        pltpu.make_async_copy(mech_ref, mech_here, arrived.at[0]),
        pltpu.make_async_copy(rate_ref, rate_here, arrived.at[1]),
    ]
    large = [
        pltpu.make_async_copy(
            green_ref.at[:, pl.ds(first, chunk), :], green_here.at[:, pl.ds(first, chunk), :], landed.at[number]
        )
        for number, first in enumerate(range(0, points, chunk))
    ]
    for copy in small + large:
        copy.start()
    blank = jnp.zeros((rows, LANES), jnp.float32)

    def clear(number, carry):
        out_ref[pl.ds(pl.multiple_of(number * 2 * rows, rows), rows), :] = blank
        return carry

    lax.fori_loop(0, 2 * points, clear, 0, unroll=8)
    flat_ref[...] = jnp.zeros_like(flat_ref)
    for copy in small:
        copy.wait()
    taps = rate_here.shape[1]
    for part in range(parts):
        for kind in range(2):
            flat_ref[2 * part + kind : 2 * part + kind + 1, :] = mech_here[part, kind : kind + 1, :]
    flat_ref[2 * parts : 2 * parts + 1, 0:taps] = rate_here[...]
    column_ref[...] = flat_ref[...].T
    rates_ref[...] = jnp.broadcast_to(column_ref[0:taps, 2 * parts : 2 * parts + 1], (taps, LANES))

    def one(number, carry):
        first = pl.multiple_of(number * group, group)
        scale = [
            jnp.broadcast_to(column_ref[pl.ds(first, group), i : i + 1], (group, LANES))
            for i in range(2 * parts)
        ]
        for step in range(rows):
            total = [jnp.zeros((group, LANES), jnp.float32)] * 2
            for part in range(parts):
                block = green_here[part, pl.ds(first, group), step * LANES : (step + 1) * LANES].astype(
                    jnp.float32
                )
                total = [total[kind] + scale[2 * part + kind] * block for kind in range(2)]
            for kind in range(2):
                kept = total[kind].astype(jnp.bfloat16).astype(jnp.float32)
                for half in range(group // 8):
                    start = (first + half * 8) * (4 * rows) + kind * 2 * rows + rows + step
                    out_ref[pl.ds(start, 8, stride=4 * rows), :] = kept[half * 8 : half * 8 + 8]
        return carry

    for number, copy in enumerate(large):
        copy.wait()
        lax.fori_loop(number * (chunk // group), (number + 1) * (chunk // group), one, 0)


def gather_kernel(capacity, rows, sent_ref, trace_ref, out_ref, word_here, word_ref, scale_ref, arrived):
    scales = pltpu.make_async_copy(sent_ref, scale_ref, arrived.at[0])
    scales.start()
    sent = sent_ref[...]
    whole = (sent + 0.5).astype(jnp.int32)
    word_here[...] = whole * LANES + pltpu.roll(whole, LANES - capacity, 1)
    words = pltpu.make_async_copy(word_here, word_ref, arrived.at[1])
    words.start()
    left = LANES - 1 - lax.broadcasted_iota(jnp.int32, (rows, LANES), 1)
    scales.wait()
    words.wait()
    for number in range(out_ref.shape[0]):
        total = [jnp.zeros((rows, LANES), jnp.float32)] * 2
        for slot in range(capacity):
            word = word_ref[number, slot]
            first = scale_ref[number, slot + 2 * capacity]
            second = scale_ref[number, slot + 3 * capacity]
            base = word // LANES
            shift = word & (LANES - 1)
            stays = left >= shift
            one_kind = jnp.where(
                stays, trace_ref[pl.ds(base + 1, rows), :], trace_ref[pl.ds(base, rows), :]
            )
            base = base + 2 * rows
            other_kind = jnp.where(
                stays, trace_ref[pl.ds(base + 1, rows), :], trace_ref[pl.ds(base, rows), :]
            )
            moved = pltpu.roll(one_kind * first + other_kind * second, shift, 1)
            total[slot % 2] = total[slot % 2] + moved
        out_ref[number] = total[0] + total[1]


def smooth_kernel(rates_ref, part_ref, out_ref):
    signal = jnp.sum(part_ref[...], axis=0)
    taps = rates_ref.shape[0]
    rows = signal.shape[0]
    row = lax.broadcasted_iota(jnp.int32, (rows, LANES), 0)
    lane = lax.broadcasted_iota(jnp.int32, (rows, LANES), 1)
    previous = jnp.where(row == 0, 0.0, pltpu.roll(signal, 1, 0))
    total = [jnp.zeros_like(signal)] * 4
    for tap in range(taps):
        moved = signal
        if tap > 0:
            moved = pltpu.roll(jnp.where(lane < LANES - tap, signal, previous), tap, 1)
        total[tap % 4] = total[tap % 4] + moved * rates_ref[tap : tap + 1, :]
    out_ref[...] = (total[0] + total[1]) + (total[2] + total[3])


def local(
    green_tensor,
    mechanism,
    point_owner,
    point_row,
    onset_step,
    slip_amount,
    point_count,
    rake_angle,
    slip_rate,
):
    owners = lax.axis_size("owner")
    variations, length = point_row.shape
    points, parts, steps = green_tensor.shape
    taps = slip_rate.shape[1]
    rows = steps // LANES
    capacity = 2 * length // owners
    assert variations == 1 and capacity * FIELDS <= LANES
    listed = [point_owner.reshape(1, length), point_row, onset_step, slip_amount, point_count, rake_angle]
    table = pl.pallas_call(
        functools.partial(route_kernel, capacity, rows),
        out_shape=jax.ShapeDtypeStruct((owners, LANES), jnp.float32),
        in_specs=[ANY] * 6,
        out_specs=VMEM,
        scratch_shapes=[pltpu.VMEM((1, length), array.dtype) for array in listed[:4]]
        + [pltpu.SMEM((1,), jnp.int32), pltpu.SMEM((1,), jnp.float32), pltpu.SemaphoreType.DMA((6,))],
        compiler_params=SMALL,
        name="route",
    )(*[in_hbm(array) for array in listed[:4]], *listed[4:])
    table = lax.all_to_all(
        table.reshape(owners, 1, LANES), "owner", split_axis=0, concat_axis=0, tiled=True
    )
    group, chunk = 16, 32
    traces, rates = pl.pallas_call(
        functools.partial(project_kernel, rows, group, chunk),
        out_shape=(
            pltpu.VMEM((points * 4 * rows, LANES), jnp.float32),
            pltpu.VMEM((taps, LANES), jnp.float32),
        ),
        in_specs=[ANY] * 3,
        out_specs=(VMEM, VMEM),
        scratch_shapes=[
            pltpu.VMEM((parts, 2, points), jnp.float32),
            pltpu.VMEM((1, taps), jnp.float32),
            pltpu.VMEM((parts, points, steps), jnp.bfloat16),
            pltpu.VMEM((LANES, points), jnp.float32),
            pltpu.VMEM((points, LANES), jnp.float32),
            pltpu.SemaphoreType.DMA((2,)),
            pltpu.SemaphoreType.DMA((points // chunk,)),
        ],
        compiler_params=SMALL,
        name="project",
    )(
        in_hbm(jnp.transpose(mechanism, (1, 0, 2))),
        in_hbm(slip_rate),
        in_hbm(jnp.transpose(green_tensor, (1, 0, 2))),
    )
    partial = pl.pallas_call(
        functools.partial(gather_kernel, capacity, rows),
        out_shape=pltpu.VMEM((owners, rows, LANES), jnp.float32),
        in_specs=[VMEM, VMEM],
        out_specs=VMEM,
        scratch_shapes=[
            pltpu.VMEM((owners, LANES), jnp.int32),
            pltpu.SMEM((owners, LANES), jnp.int32),
            pltpu.SMEM((owners, LANES), jnp.float32),
            pltpu.SemaphoreType.DMA((2,)),
        ],
        compiler_params=SMALL,
        name="gather",
    )(in_vmem(table.reshape(owners, LANES)), in_vmem(traces))
    partial = lax.all_to_all(partial, "owner", split_axis=0, concat_axis=0, tiled=True)
    result = pl.pallas_call(
        smooth_kernel,
        out_shape=jax.ShapeDtypeStruct((rows, LANES), jnp.float32),
        in_specs=[VMEM, VMEM],
        out_specs=VMEM,
        compiler_params=SMALL,
        name="smooth",
    )(in_vmem(rates), in_vmem(partial))
    return result.reshape(1, steps)


def solution(mesh):
    in_specs = (
        P(("site", "owner"), None, None),
        P(None, None, "owner"),
        P("owner", None, None),
        P("owner", None),
        P("owner", None),
        P("owner", None),
        P("owner"),
        P("owner"),
        P("owner", None),
    )
    out_specs = P(("site", "owner"), None)
    return jax.shard_map(local, mesh=mesh, in_specs=in_specs, out_specs=out_specs, check_vma=False)
```

time: 35.7 us -> 29.7 us (0.83)
  Pallas kernels: 13.1 us -> 7.78 us
  blocking collectives: 11.6 us -> 9.48 us
  waiting for transfers between devices: 1.45 us -> 3.43 us
  local copies, waits for them, and re-layouts: 0.59 us -> 0 us
    pallas_call x2, Pallas kernels: 6.58 us -> 3.75 us  [the longest x1 3 us: local(): pl.pallas_call(functools.partial(project_kernel, rows, group, chunk), out...]
    pallas_call x1, Pallas kernels: 4.83 us -> 2.3 us  [local(): pl.pallas_call(functools.partial(gather_kernel, capacity, rows), out_shap...]
    all_to_all x1, blocking collectives: 11.6 us -> 9.48 us  [local(): lax.all_to_all(partial, 'owner', split_axis=0, concat_axis=0, tiled=True)]
    all_to_all x1, waiting for transfers between devices: 1.45 us -> 3.43 us  [local(): lax.all_to_all(table.reshape(owners, 1, LANES), 'owner', split_axis=0, co...]
    unnamed x2 -> x0, local copies, waits for them, and re-layouts: 0.59 us -> none
  transfers between devices with their start and end apart: 1 -> 1, of which waited for: 1 -> 1; matrix products, arithmetic and copies ran while one was open for 0% -> 0% of each run, Pallas kernels for 14% -> 10%
where the time goes in v2:
time: 29.7 us; the launch traced here: 29.4 us
  blocking collectives  9.48 us (32%)
  Pallas kernels  7.78 us (26%)
  starting transfers between devices  7.4 us (25%)
  waiting for transfers between devices  3.43 us (12%)
  between operations  1.33 us (4%)
    all_to_all x1, blocking collectives, local(): lax.all_to_all(partial, 'owner', split_axis=0, concat_axis=0, tiled=True)  9.48 us
    all_to_all x1, starting transfers between devices, local(): lax.all_to_all(table.reshape(owners, 1, LANES), 'owner', split_axis=0, co...  7.4 us
    all_to_all x1, waiting for transfers between devices, local(): lax.all_to_all(table.reshape(owners, 1, LANES), 'owner', split_axis=0, co...  3.43 us
    pallas_call x1, Pallas kernels, local(): pl.pallas_call(functools.partial(project_kernel, rows, group, chunk), out...  3 us
    pallas_call x1, Pallas kernels, local(): pl.pallas_call(functools.partial(gather_kernel, capacity, rows), out_shap...  2.3 us
    pallas_call x1, Pallas kernels, local(): pl.pallas_call(functools.partial(route_kernel, capacity, rows), out_shape...  1.73 us
    pallas_call x1, Pallas kernels, local(): pl.pallas_call(smooth_kernel, out_shape=jax.ShapeDtypeStruct((rows, LANES...  0.75 us
  transfers between devices with their start and end apart: 1, of which 1 were waited for; matrix products, arithmetic and copies ran while one was open for 0% of the time, Pallas kernels for 10%

profile of v2, /device:TPU:0, one launch (start us, length us, event | category | flops | bytes accessed | tf_op | source)
XLA Modules:
  0.0 29.4 jit_solution(2380958478268312623)
XLA Ops:
  1.3 1.7 %route.1 = f32[16,128]{1,0:T(8,128)} custom-call(s32[1,128]{1,0:T(1,128)} %bitcast.11, s32[1,128]{1,0:T(1,128)} %refs_1_.1, s32[1,128]{1,0:T(1,128)} %refs_2_.1, f32[1,128]{1,0:T(1,128)} %refs_3_.1, s32[1]{0:T(128)S(6)} %copy.11.refs_4_, f32[1]{0:T(128)S(6)} %copy.12.refs_5_), custom_call_target="tpu_custom_call" | custom-call | tf_op jit(solution)/shard_map/route/pallas_call | solution.py:202
  3.0 7.4 %all-to-all-start = ((f32[16,1,128]{2,1,0:T(1,128)}), f32[16,1,128]{2,1,0:T(1,128)S(1)}, u32[]{:S(2)}, u32[]{:S(2)}) async-start(f32[16,1,128]{2,1,0:T(1,128)} %bitcast.4), calls=%async_computation | async-start | bytes 16384 | tf_op jit(solution)/shard_map/all_to_all | solution.py:212
  10.4 3.0 %project.1 = (f32[4096,128]{1,0:T(8,128)S(1)}, f32[64,128]{1,0:T(8,128)S(1)}) custom-call(f32[6,2,128]{2,1,0:T(2,128)} %bitcast.10, f32[1,64]{1,0:T(1,128)} %rate_ref.1, bf16[6,128,1024]{2,1,0:T(8,128)(2,1)} %bitcast.9), custom_call_target="tpu_custom_call" | custom-call | tf_op jit(solution)/shard_map/project/pallas_call | solution.py:216
  13.5 3.4 %all-to-all-done = f32[16,1,128]{2,1,0:T(1,128)S(1)} async-done(((f32[16,1,128]{2,1,0:T(1,128)}), f32[16,1,128]{2,1,0:T(1,128)S(1)}, u32[]{:S(2)}, u32[]{:S(2)}) %all-to-all-start) | async-done | bytes 8224 | tf_op jit(solution)/shard_map/all_to_all | solution.py:212
  16.9 2.3 %gather.1 = f32[16,8,128]{2,1,0:T(8,128)S(1)} custom-call(f32[16,128]{1,0:T(8,128)S(1)} %bitcast.8, f32[4096,128]{1,0:T(8,128)S(1)} %get-tuple-element.8.trace_ref), custom_call_target="tpu_custom_call" | custom-call | tf_op jit(solution)/shard_map/gather/pallas_call | solution.py:240
  19.2 9.5 %all_to_all.10.part_ref = f32[16,8,128]{2,1,0:T(8,128)S(1)} all-to-all(f32[16,8,128]{2,1,0:T(8,128)S(1)} %gather.1), channel_id=1, replica_groups=mesh['site'=2,'owner'=16] {'owner'}, dimensions={0} | all-to-all | bytes 131072 | tf_op jit(solution)/shard_map/all_to_all | solution.py:254
  28.7 0.7 %smooth.1 = f32[8,128]{1,0:T(8,128)} custom-call(f32[64,128]{1,0:T(8,128)S(1)} %get-tuple-element.7.rates_ref, f32[16,8,128]{2,1,0:T(8,128)S(1)} %all_to_all.10.part_ref), custom_call_target="tpu_custom_call" | custom-call | tf_op jit(solution)/shard_map/smooth/pallas_call | solution.py:255
Async XLA Ops:
  3.0 13.8 %all-to-all-start = ((f32[16,1,128]{2,1,0:T(1,128)}), f32[16,1,128]{2,1,0:T(1,128)S(1)}, u32[]{:S(2)}, u32[]{:S(2)}) async-start(f32[16,1,128]{2,1,0:T(1,128)} %bitcast.4), calls=%async_computation | async-start | bytes 16384 | tf_op jit(solution)/shard_map/all_to_all | solution.py:212

commit v3 on v2

--- a/solution.py
+++ b/solution.py
@@ -10,6 +10,7 @@
 LANES = 128
 FIELDS = 4
 ANY = pl.BlockSpec(memory_space=pltpu.HBM)
+SMEM = pl.BlockSpec(memory_space=pltpu.SMEM)
 VMEM = pl.BlockSpec(memory_space=pltpu.VMEM)
 SMALL = pltpu.CompilerParams(vmem_limit_bytes=16 << 20)
 
@@ -34,9 +35,11 @@
 
 
 def route_kernel(capacity, rows, *refs):
-    sources, out_ref, targets, arrived = refs[:6], refs[6], refs[7:13], refs[13]
+    count_ref, rake_ref, sources, out_ref, targets, arrived = (
+        refs[0], refs[1], refs[2:6], refs[6], refs[7:11], refs[11]
+    )
     fetch(sources, targets, arrived)
-    owner_ref, row_ref, onset_ref, slip_ref, count_ref, rake_ref = targets
+    owner_ref, row_ref, onset_ref, slip_ref = targets
     owners = out_ref.shape[0]
     length = row_ref.shape[1]
     lane = lax.broadcasted_iota(jnp.int32, (1, length), 1)
@@ -149,7 +152,7 @@
             word = word_ref[number, slot]
             first = scale_ref[number, slot + 2 * capacity]
             second = scale_ref[number, slot + 3 * capacity]
-            base = word // LANES
+            base = word >> (LANES.bit_length() - 1)
             shift = word & (LANES - 1)
             stays = left >= shift
             one_kind = jnp.where(
@@ -198,17 +201,17 @@
     rows = steps // LANES
     capacity = 2 * length // owners
     assert variations == 1 and capacity * FIELDS <= LANES
-    listed = [point_owner.reshape(1, length), point_row, onset_step, slip_amount, point_count, rake_angle]
+    listed = [point_owner.reshape(1, length), point_row, onset_step, slip_amount]
     table = pl.pallas_call(
         functools.partial(route_kernel, capacity, rows),
         out_shape=jax.ShapeDtypeStruct((owners, LANES), jnp.float32),
-        in_specs=[ANY] * 6,
+        in_specs=[SMEM] * 2 + [ANY] * 4,
         out_specs=VMEM,
-        scratch_shapes=[pltpu.VMEM((1, length), array.dtype) for array in listed[:4]]
-        + [pltpu.SMEM((1,), jnp.int32), pltpu.SMEM((1,), jnp.float32), pltpu.SemaphoreType.DMA((6,))],
+        scratch_shapes=[pltpu.VMEM((1, length), array.dtype) for array in listed]
+        + [pltpu.SemaphoreType.DMA((4,))],
         compiler_params=SMALL,
         name="route",
-    )(*[in_hbm(array) for array in listed[:4]], *listed[4:])
+    )(point_count, rake_angle, *[in_hbm(array) for array in listed])
     table = lax.all_to_all(
         table.reshape(owners, 1, LANES), "owner", split_axis=0, concat_axis=0, tiled=True
     )

time: 29.7 us -> 28.6 us (0.963)
  Pallas kernels: 7.78 us -> 6.74 us
    pallas_call x1, Pallas kernels: 2.3 us -> 1.29 us  [local(): pl.pallas_call(functools.partial(gather_kernel, capacity, rows), out_shap...]
  transfers between devices with their start and end apart: 1 -> 1, of which waited for: 1 -> 1; matrix products, arithmetic and copies ran while one was open for 0% -> 0% of each run, Pallas kernels for 10% -> 11%
where the time goes in v3:
time: 28.6 us; the launch traced here: 28.4 us
  blocking collectives  9.48 us (33%)
  starting transfers between devices  7.4 us (26%)
  Pallas kernels  6.74 us (24%)
  waiting for transfers between devices  3.43 us (12%)
  between operations  1.33 us (5%)
    all_to_all x1, blocking collectives, local(): lax.all_to_all(partial, 'owner', split_axis=0, concat_axis=0, tiled=True)  9.48 us
    all_to_all x1, starting transfers between devices, local(): lax.all_to_all(table.reshape(owners, 1, LANES), 'owner', split_axis=0, co...  7.4 us
    all_to_all x1, waiting for transfers between devices, local(): lax.all_to_all(table.reshape(owners, 1, LANES), 'owner', split_axis=0, co...  3.43 us
    pallas_call x1, Pallas kernels, local(): pl.pallas_call(functools.partial(project_kernel, rows, group, chunk), out...  3 us
    pallas_call x1, Pallas kernels, local(): pl.pallas_call(functools.partial(route_kernel, capacity, rows), out_shape...  1.7 us
    pallas_call x1, Pallas kernels, local(): pl.pallas_call(functools.partial(gather_kernel, capacity, rows), out_shap...  1.29 us
    pallas_call x1, Pallas kernels, local(): pl.pallas_call(smooth_kernel, out_shape=jax.ShapeDtypeStruct((rows, LANES...  0.75 us
  transfers between devices with their start and end apart: 1, of which 1 were waited for; matrix products, arithmetic and copies ran while one was open for 0% of the time, Pallas kernels for 11%

profile of v3, /device:TPU:0, one launch (start us, length us, event | category | flops | bytes accessed | tf_op | source)
XLA Modules:
  0.0 28.4 jit_solution(957655465471480756)
XLA Ops:
  1.3 1.7 %route.1 = f32[16,128]{1,0:T(8,128)} custom-call(s32[1]{0:T(128)S(6)} %copy.11.refs_0_, f32[1]{0:T(128)S(6)} %copy.12.refs_1_, s32[1,128]{1,0:T(1,128)} %bitcast.11, s32[1,128]{1,0:T(1,128)} %refs_3_.1, s32[1,128]{1,0:T(1,128)} %refs_4_.1, f32[1,128]{1,0:T(1,128)} %refs_5_.1), custom_call_target="tpu_custom_call" | custom-call | tf_op jit(solution)/shard_map/route/pallas_call | solution.py:205
  3.0 7.4 %all-to-all-start = ((f32[16,1,128]{2,1,0:T(1,128)}), f32[16,1,128]{2,1,0:T(1,128)S(1)}, u32[]{:S(2)}, u32[]{:S(2)}) async-start(f32[16,1,128]{2,1,0:T(1,128)} %bitcast.4), calls=%async_computation | async-start | bytes 16384 | tf_op jit(solution)/shard_map/all_to_all | solution.py:215
  10.4 3.0 %project.1 = (f32[4096,128]{1,0:T(8,128)S(1)}, f32[64,128]{1,0:T(8,128)S(1)}) custom-call(f32[6,2,128]{2,1,0:T(2,128)} %bitcast.10, f32[1,64]{1,0:T(1,128)} %rate_ref.1, bf16[6,128,1024]{2,1,0:T(8,128)(2,1)} %bitcast.9), custom_call_target="tpu_custom_call" | custom-call | tf_op jit(solution)/shard_map/project/pallas_call | solution.py:219
  13.4 3.4 %all-to-all-done = f32[16,1,128]{2,1,0:T(1,128)S(1)} async-done(((f32[16,1,128]{2,1,0:T(1,128)}), f32[16,1,128]{2,1,0:T(1,128)S(1)}, u32[]{:S(2)}, u32[]{:S(2)}) %all-to-all-start) | async-done | bytes 8224 | tf_op jit(solution)/shard_map/all_to_all | solution.py:215
  16.8 1.3 %gather.1 = f32[16,8,128]{2,1,0:T(8,128)S(1)} custom-call(f32[16,128]{1,0:T(8,128)S(1)} %bitcast.8, f32[4096,128]{1,0:T(8,128)S(1)} %get-tuple-element.8.trace_ref), custom_call_target="tpu_custom_call" | custom-call | tf_op jit(solution)/shard_map/gather/pallas_call | solution.py:243
  18.1 9.5 %all_to_all.10.part_ref = f32[16,8,128]{2,1,0:T(8,128)S(1)} all-to-all(f32[16,8,128]{2,1,0:T(8,128)S(1)} %gather.1), channel_id=1, replica_groups=mesh['site'=2,'owner'=16] {'owner'}, dimensions={0} | all-to-all | bytes 131072 | tf_op jit(solution)/shard_map/all_to_all | solution.py:257
  27.6 0.7 %smooth.1 = f32[8,128]{1,0:T(8,128)} custom-call(f32[64,128]{1,0:T(8,128)S(1)} %get-tuple-element.7.rates_ref, f32[16,8,128]{2,1,0:T(8,128)S(1)} %all_to_all.10.part_ref), custom_call_target="tpu_custom_call" | custom-call | tf_op jit(solution)/shard_map/smooth/pallas_call | solution.py:258
Async XLA Ops:
  3.0 13.8 %all-to-all-start = ((f32[16,1,128]{2,1,0:T(1,128)}), f32[16,1,128]{2,1,0:T(1,128)S(1)}, u32[]{:S(2)}, u32[]{:S(2)}) async-start(f32[16,1,128]{2,1,0:T(1,128)} %bitcast.4), calls=%async_computation | async-start | bytes 16384 | tf_op jit(solution)/shard_map/all_to_all | solution.py:215

commit v4 on v3

--- a/solution.py
+++ b/solution.py
@@ -44,35 +44,48 @@
     length = row_ref.shape[1]
     lane = lax.broadcasted_iota(jnp.int32, (1, length), 1)
     alive = lane < count_ref[0]
+    owner_index = lax.broadcasted_iota(jnp.int32, (owners, length), 0)
+    hot = ((owner_index == owner_ref[...]) & alive).astype(jnp.float32)
+    earlier = lax.broadcasted_iota(jnp.int32, (length, length), 0) < lax.broadcasted_iota(
+        jnp.int32, (length, length), 1
+    )
+    before = jnp.dot(
+        hot.astype(jnp.bfloat16), earlier.astype(jnp.bfloat16), preferred_element_type=jnp.float32
+    )
+    rank = jnp.sum(hot * before, axis=0, keepdims=True).astype(jnp.int32)
     onset = onset_ref[...]
-    whole = onset // LANES
+    whole = onset >> (LANES.bit_length() - 1)
     base = row_ref[...] * (4 * rows) + (rows - 1) - whole
     rake = jnp.full((1, length), rake_ref[0], jnp.float32)
     weight = jnp.where(alive, slip_ref[...], 0.0)
     fields = (
         base.astype(jnp.float32),
-        (onset - whole * LANES).astype(jnp.float32),
+        (onset & (LANES - 1)).astype(jnp.float32),
         jnp.cos(rake) * weight,
         jnp.sin(rake) * weight,
     )
-    owner_index = lax.broadcasted_iota(jnp.int32, (owners, length), 0)
-    hot = ((owner_index == owner_ref[...]) & alive).astype(jnp.float32)
-    earlier = lax.broadcasted_iota(jnp.int32, (length, length), 0) < lax.broadcasted_iota(
-        jnp.int32, (length, length), 1
-    )
-    before = jnp.dot(hot, earlier.astype(jnp.float32), preferred_element_type=jnp.float32)
-    rank = jnp.sum(hot * before, axis=0, keepdims=True).astype(jnp.int32)
-    place = lax.broadcasted_iota(jnp.int32, (LANES, length), 0)
-    spread = jnp.zeros((LANES, length), jnp.float32)
-    for number, field in enumerate(fields):
-        spread = jnp.where(place == rank + number * capacity, field, spread)
-    out_ref[...] = lax.dot_general(
-        hot,
-        spread,
-        (((1,), (1,)), ((), ())),
-        precision=lax.Precision.HIGHEST,
-        preferred_element_type=jnp.float32,
-    )
+    place = lax.broadcasted_iota(jnp.int32, (len(fields) * capacity, length), 0)
+    pieces = []
+    for field in fields:
+        piece = []
+        for _ in range(3):
+            piece.append(field.astype(jnp.bfloat16).astype(jnp.float32))
+            field = field - piece[-1]
+        pieces.append(piece)
+    total = None
+    for part in range(3):
+        spread = jnp.zeros(place.shape, jnp.float32)
+        for number, piece in enumerate(pieces):
+            spread = jnp.where(place == rank + number * capacity, piece[part], spread)
+        term = lax.dot_general(
+            hot.astype(jnp.bfloat16),
+            spread.astype(jnp.bfloat16),
+            (((1,), (1,)), ((), ())),
+            preferred_element_type=jnp.float32,
+        )
+        total = term if part == 0 else total + term
+    out_ref[...] = jnp.zeros_like(out_ref)
+    out_ref[:, 0 : total.shape[1]] = total
 
 
 def project_kernel(
@@ -138,9 +151,7 @@
 def gather_kernel(capacity, rows, sent_ref, trace_ref, out_ref, word_here, word_ref, scale_ref, arrived):
     scales = pltpu.make_async_copy(sent_ref, scale_ref, arrived.at[0])
     scales.start()
-    sent = sent_ref[...]
-    whole = (sent + 0.5).astype(jnp.int32)
-    word_here[...] = whole * LANES + pltpu.roll(whole, LANES - capacity, 1)
+    word_here[...] = (sent_ref[...] + 0.5).astype(jnp.int32)
     words = pltpu.make_async_copy(word_here, word_ref, arrived.at[1])
     words.start()
     left = LANES - 1 - lax.broadcasted_iota(jnp.int32, (rows, LANES), 1)
@@ -149,11 +160,10 @@
     for number in range(out_ref.shape[0]):
         total = [jnp.zeros((rows, LANES), jnp.float32)] * 2
         for slot in range(capacity):
-            word = word_ref[number, slot]
+            base = word_ref[number, slot]
+            shift = word_ref[number, slot + capacity]
             first = scale_ref[number, slot + 2 * capacity]
             second = scale_ref[number, slot + 3 * capacity]
-            base = word >> (LANES.bit_length() - 1)
-            shift = word & (LANES - 1)
             stays = left >= shift
             one_kind = jnp.where(
                 stays, trace_ref[pl.ds(base + 1, rows), :], trace_ref[pl.ds(base, rows), :]

time: 28.6 us -> 28.5 us (level)
  no operation moved by 1% of the time
where the time goes in v4:
time: 28.5 us; the launch traced here: 28.3 us
  blocking collectives  9.48 us (33%)
  starting transfers between devices  7.4 us (26%)
  Pallas kernels  6.67 us (23%)
  waiting for transfers between devices  3.43 us (12%)
  between operations  1.33 us (5%)
    all_to_all x1, blocking collectives, local(): lax.all_to_all(partial, 'owner', split_axis=0, concat_axis=0, tiled=True)  9.48 us
    all_to_all x1, starting transfers between devices, local(): lax.all_to_all(table.reshape(owners, 1, LANES), 'owner', split_axis=0, co...  7.4 us
    all_to_all x1, waiting for transfers between devices, local(): lax.all_to_all(table.reshape(owners, 1, LANES), 'owner', split_axis=0, co...  3.43 us
    pallas_call x1, Pallas kernels, local(): pl.pallas_call(functools.partial(project_kernel, rows, group, chunk), out...  3 us
    pallas_call x1, Pallas kernels, local(): pl.pallas_call(functools.partial(route_kernel, capacity, rows), out_shape...  1.63 us
    pallas_call x1, Pallas kernels, local(): pl.pallas_call(functools.partial(gather_kernel, capacity, rows), out_shap...  1.29 us
    pallas_call x1, Pallas kernels, local(): pl.pallas_call(smooth_kernel, out_shape=jax.ShapeDtypeStruct((rows, LANES...  0.75 us
  transfers between devices with their start and end apart: 1, of which 1 were waited for; matrix products, arithmetic and copies ran while one was open for 0% of the time, Pallas kernels for 11%

profile of v4, /device:TPU:0, one launch (start us, length us, event | category | flops | bytes accessed | tf_op | source)
XLA Modules:
  0.0 28.3 jit_solution(4971405452550400983)
XLA Ops:
  1.3 1.6 %route.1 = f32[16,128]{1,0:T(8,128)} custom-call(s32[1]{0:T(128)S(6)} %copy.11.refs_0_, f32[1]{0:T(128)S(6)} %copy.12.refs_1_, s32[1,128]{1,0:T(1,128)} %bitcast.11, s32[1,128]{1,0:T(1,128)} %refs_3_.1, s32[1,128]{1,0:T(1,128)} %refs_4_.1, f32[1,128]{1,0:T(1,128)} %refs_5_.1), custom_call_target="tpu_custom_call" | custom-call | tf_op jit(solution)/shard_map/route/pallas_call | solution.py:215
  2.9 7.4 %all-to-all-start = ((f32[16,1,128]{2,1,0:T(1,128)}), f32[16,1,128]{2,1,0:T(1,128)S(1)}, u32[]{:S(2)}, u32[]{:S(2)}) async-start(f32[16,1,128]{2,1,0:T(1,128)} %bitcast.4), calls=%async_computation | async-start | bytes 16384 | tf_op jit(solution)/shard_map/all_to_all | solution.py:225
  10.3 3.0 %project.1 = (f32[4096,128]{1,0:T(8,128)S(1)}, f32[64,128]{1,0:T(8,128)S(1)}) custom-call(f32[6,2,128]{2,1,0:T(2,128)} %bitcast.10, f32[1,64]{1,0:T(1,128)} %rate_ref.1, bf16[6,128,1024]{2,1,0:T(8,128)(2,1)} %bitcast.9), custom_call_target="tpu_custom_call" | custom-call | tf_op jit(solution)/shard_map/project/pallas_call | solution.py:229
  13.4 3.4 %all-to-all-done = f32[16,1,128]{2,1,0:T(1,128)S(1)} async-done(((f32[16,1,128]{2,1,0:T(1,128)}), f32[16,1,128]{2,1,0:T(1,128)S(1)}, u32[]{:S(2)}, u32[]{:S(2)}) %all-to-all-start) | async-done | bytes 8224 | tf_op jit(solution)/shard_map/all_to_all | solution.py:225
  16.8 1.3 %gather.1 = f32[16,8,128]{2,1,0:T(8,128)S(1)} custom-call(f32[16,128]{1,0:T(8,128)S(1)} %bitcast.8, f32[4096,128]{1,0:T(8,128)S(1)} %get-tuple-element.8.trace_ref), custom_call_target="tpu_custom_call" | custom-call | tf_op jit(solution)/shard_map/gather/pallas_call | solution.py:253
  18.1 9.5 %all_to_all.10.part_ref = f32[16,8,128]{2,1,0:T(8,128)S(1)} all-to-all(f32[16,8,128]{2,1,0:T(8,128)S(1)} %gather.1), channel_id=1, replica_groups=mesh['site'=2,'owner'=16] {'owner'}, dimensions={0} | all-to-all | bytes 131072 | tf_op jit(solution)/shard_map/all_to_all | solution.py:267
  27.6 0.7 %smooth.1 = f32[8,128]{1,0:T(8,128)} custom-call(f32[64,128]{1,0:T(8,128)S(1)} %get-tuple-element.7.rates_ref, f32[16,8,128]{2,1,0:T(8,128)S(1)} %all_to_all.10.part_ref), custom_call_target="tpu_custom_call" | custom-call | tf_op jit(solution)/shard_map/smooth/pallas_call | solution.py:268
Async XLA Ops:
  2.9 13.8 %all-to-all-start = ((f32[16,1,128]{2,1,0:T(1,128)}), f32[16,1,128]{2,1,0:T(1,128)S(1)}, u32[]{:S(2)}, u32[]{:S(2)}) async-start(f32[16,1,128]{2,1,0:T(1,128)} %bitcast.4), calls=%async_computation | async-start | bytes 16384 | tf_op jit(solution)/shard_map/all_to_all | solution.py:225

commit v5 on v4

--- a/solution.py
+++ b/solution.py
@@ -55,7 +55,7 @@
     rank = jnp.sum(hot * before, axis=0, keepdims=True).astype(jnp.int32)
     onset = onset_ref[...]
     whole = onset >> (LANES.bit_length() - 1)
-    base = row_ref[...] * (4 * rows) + (rows - 1) - whole
+    base = row_ref[...] * (4 * rows + 1) + (rows - 1) - whole
     rake = jnp.full((1, length), rake_ref[0], jnp.float32)
     weight = jnp.where(alive, slip_ref[...], 0.0)
     fields = (
@@ -105,13 +105,15 @@
     ]
     for copy in small + large:
         copy.start()
+    pitch = 4 * rows + 1
     blank = jnp.zeros((rows, LANES), jnp.float32)
 
     def clear(number, carry):
-        out_ref[pl.ds(pl.multiple_of(number * 2 * rows, rows), rows), :] = blank
+        for kind in range(2):
+            out_ref[pl.ds(number * pitch + kind * 2 * rows, rows), :] = blank
         return carry
 
-    lax.fori_loop(0, 2 * points, clear, 0, unroll=8)
+    lax.fori_loop(0, points, clear, 0, unroll=8)
     flat_ref[...] = jnp.zeros_like(flat_ref)
     for copy in small:
         copy.wait()
@@ -125,22 +127,23 @@
 
     def one(number, carry):
         first = pl.multiple_of(number * group, group)
-        scale = [
-            jnp.broadcast_to(column_ref[pl.ds(first, group), i : i + 1], (group, LANES))
-            for i in range(2 * parts)
-        ]
-        for step in range(rows):
-            total = [jnp.zeros((group, LANES), jnp.float32)] * 2
-            for part in range(parts):
-                block = green_here[part, pl.ds(first, group), step * LANES : (step + 1) * LANES].astype(
-                    jnp.float32
-                )
-                total = [total[kind] + scale[2 * part + kind] * block for kind in range(2)]
-            for kind in range(2):
-                kept = total[kind].astype(jnp.bfloat16).astype(jnp.float32)
-                for half in range(group // 8):
-                    start = (first + half * 8) * (4 * rows) + kind * 2 * rows + rows + step
-                    out_ref[pl.ds(start, 8, stride=4 * rows), :] = kept[half * 8 : half * 8 + 8]
+        for half in range(0, group, 8):
+            corner = (first + half) * pitch + rows
+            scale = [
+                jnp.broadcast_to(column_ref[pl.ds(first + half, 8), i : i + 1], (8, LANES))
+                for i in range(2 * parts)
+            ]
+            for step in range(rows):
+                total = [None, None]
+                for part in range(parts):
+                    block = green_here[part, pl.ds(first, group), step * LANES : (step + 1) * LANES]
+                    block = block.astype(jnp.float32)[half : half + 8]
+                    for kind in range(2):
+                        term = scale[2 * part + kind] * block
+                        total[kind] = term if part == 0 else total[kind] + term
+                for kind in range(2):
+                    kept = total[kind].astype(jnp.bfloat16).astype(jnp.float32)
+                    out_ref[pl.ds(corner + 2 * kind * rows + step, 8, stride=pitch), :] = kept
         return carry
 
     for number, copy in enumerate(large):
@@ -229,7 +232,7 @@
     traces, rates = pl.pallas_call(
         functools.partial(project_kernel, rows, group, chunk),
         out_shape=(
-            pltpu.VMEM((points * 4 * rows, LANES), jnp.float32),
+            pltpu.VMEM((points * (4 * rows + 1), LANES), jnp.float32),
             pltpu.VMEM((taps, LANES), jnp.float32),
         ),
         in_specs=[ANY] * 3,

time: 28.5 us -> 28.5 us (level)
  Pallas kernels: 6.67 us -> 5.96 us
  waiting for transfers between devices: 3.43 us -> 4.14 us
    all_to_all x1, waiting for transfers between devices: 3.43 us -> 4.14 us  [local(): lax.all_to_all(table.reshape(owners, 1, LANES), 'owner', split_axis=0, co...]
    pallas_call x1, Pallas kernels: 3 us -> 2.29 us  [local(): pl.pallas_call(functools.partial(project_kernel, rows, group, chunk), out...]
  transfers between devices with their start and end apart: 1 -> 1, of which waited for: 1 -> 1; matrix products, arithmetic and copies ran while one was open for 0% -> 0% of each run, Pallas kernels for 11% -> 8%
where the time goes in v5:
time: 28.5 us; the launch traced here: 28.3 us
  blocking collectives  9.48 us (33%)
  starting transfers between devices  7.4 us (26%)
  Pallas kernels  5.96 us (21%)
  waiting for transfers between devices  4.14 us (15%)
  between operations  1.33 us (5%)
    all_to_all x1, blocking collectives, local(): lax.all_to_all(partial, 'owner', split_axis=0, concat_axis=0, tiled=True)  9.48 us
    all_to_all x1, starting transfers between devices, local(): lax.all_to_all(table.reshape(owners, 1, LANES), 'owner', split_axis=0, co...  7.4 us
    all_to_all x1, waiting for transfers between devices, local(): lax.all_to_all(table.reshape(owners, 1, LANES), 'owner', split_axis=0, co...  4.14 us
    pallas_call x1, Pallas kernels, local(): pl.pallas_call(functools.partial(project_kernel, rows, group, chunk), out...  2.29 us
    pallas_call x1, Pallas kernels, local(): pl.pallas_call(functools.partial(route_kernel, capacity, rows), out_shape...  1.63 us
    pallas_call x1, Pallas kernels, local(): pl.pallas_call(functools.partial(gather_kernel, capacity, rows), out_shap...  1.29 us
    pallas_call x1, Pallas kernels, local(): pl.pallas_call(smooth_kernel, out_shape=jax.ShapeDtypeStruct((rows, LANES...  0.75 us
  transfers between devices with their start and end apart: 1, of which 1 were waited for; matrix products, arithmetic and copies ran while one was open for 0% of the time, Pallas kernels for 8%

profile of v5, /device:TPU:0, one launch (start us, length us, event | category | flops | bytes accessed | tf_op | source)
XLA Modules:
  0.0 28.3 jit_solution(18124850914477851703)
XLA Ops:
  1.3 1.6 %route.1 = f32[16,128]{1,0:T(8,128)} custom-call(s32[1]{0:T(128)S(6)} %copy.11.refs_0_, f32[1]{0:T(128)S(6)} %copy.12.refs_1_, s32[1,128]{1,0:T(1,128)} %bitcast.11, s32[1,128]{1,0:T(1,128)} %refs_3_.1, s32[1,128]{1,0:T(1,128)} %refs_4_.1, f32[1,128]{1,0:T(1,128)} %refs_5_.1), custom_call_target="tpu_custom_call" | custom-call | tf_op jit(solution)/shard_map/route/pallas_call | solution.py:218
  2.9 7.4 %all-to-all-start = ((f32[16,1,128]{2,1,0:T(1,128)}), f32[16,1,128]{2,1,0:T(1,128)S(1)}, u32[]{:S(2)}, u32[]{:S(2)}) async-start(f32[16,1,128]{2,1,0:T(1,128)} %bitcast.4), calls=%async_computation | async-start | bytes 16384 | tf_op jit(solution)/shard_map/all_to_all | solution.py:228
  10.3 2.3 %project.1 = (f32[4224,128]{1,0:T(8,128)S(1)}, f32[64,128]{1,0:T(8,128)S(1)}) custom-call(f32[6,2,128]{2,1,0:T(2,128)} %bitcast.10, f32[1,64]{1,0:T(1,128)} %rate_ref.1, bf16[6,128,1024]{2,1,0:T(8,128)(2,1)} %bitcast.9), custom_call_target="tpu_custom_call" | custom-call | tf_op jit(solution)/shard_map/project/pallas_call | solution.py:232
  12.6 4.1 %all-to-all-done = f32[16,1,128]{2,1,0:T(1,128)S(1)} async-done(((f32[16,1,128]{2,1,0:T(1,128)}), f32[16,1,128]{2,1,0:T(1,128)S(1)}, u32[]{:S(2)}, u32[]{:S(2)}) %all-to-all-start) | async-done | bytes 8224 | tf_op jit(solution)/shard_map/all_to_all | solution.py:228
  16.8 1.3 %gather.1 = f32[16,8,128]{2,1,0:T(8,128)S(1)} custom-call(f32[16,128]{1,0:T(8,128)S(1)} %bitcast.8, f32[4224,128]{1,0:T(8,128)S(1)} %get-tuple-element.8.trace_ref), custom_call_target="tpu_custom_call" | custom-call | tf_op jit(solution)/shard_map/gather/pallas_call | solution.py:256
  18.1 9.5 %all_to_all.10.part_ref = f32[16,8,128]{2,1,0:T(8,128)S(1)} all-to-all(f32[16,8,128]{2,1,0:T(8,128)S(1)} %gather.1), channel_id=1, replica_groups=mesh['site'=2,'owner'=16] {'owner'}, dimensions={0} | all-to-all | bytes 131072 | tf_op jit(solution)/shard_map/all_to_all | solution.py:270
  27.6 0.7 %smooth.1 = f32[8,128]{1,0:T(8,128)} custom-call(f32[64,128]{1,0:T(8,128)S(1)} %get-tuple-element.7.rates_ref, f32[16,8,128]{2,1,0:T(8,128)S(1)} %all_to_all.10.part_ref), custom_call_target="tpu_custom_call" | custom-call | tf_op jit(solution)/shard_map/smooth/pallas_call | solution.py:271
Async XLA Ops:
  2.9 13.8 %all-to-all-start = ((f32[16,1,128]{2,1,0:T(1,128)}), f32[16,1,128]{2,1,0:T(1,128)S(1)}, u32[]{:S(2)}, u32[]{:S(2)}) async-start(f32[16,1,128]{2,1,0:T(1,128)} %bitcast.4), calls=%async_computation | async-start | bytes 16384 | tf_op jit(solution)/shard_map/all_to_all | solution.py:228

commit v6 on v5

--- a/solution.py
+++ b/solution.py
@@ -23,46 +23,42 @@
     return pltpu.with_memory_space_constraint(array, pltpu.VMEM)
 
 
-def fetch(sources, targets, arrived):
+def route_kernel(capacity, rows, *refs):
+    count_ref, rake_ref, sources, out_ref, targets, arrived = (
+        refs[0], refs[1], refs[2:6], refs[6], refs[7:11], refs[11]
+    )
+    turn_ref, earlier_ref = refs[12:]
     copies = [
         pltpu.make_async_copy(source, target, arrived.at[number])
         for number, (source, target) in enumerate(zip(sources, targets))
     ]
     for copy in copies:
         copy.start()
-    for copy in copies:
-        copy.wait()
-
-
-def route_kernel(capacity, rows, *refs):
-    count_ref, rake_ref, sources, out_ref, targets, arrived = (
-        refs[0], refs[1], refs[2:6], refs[6], refs[7:11], refs[11]
-    )
-    fetch(sources, targets, arrived)
     owner_ref, row_ref, onset_ref, slip_ref = targets
     owners = out_ref.shape[0]
     length = row_ref.shape[1]
-    lane = lax.broadcasted_iota(jnp.int32, (1, length), 1)
-    alive = lane < count_ref[0]
+    out_ref[...] = jnp.zeros_like(out_ref)
+    alive = lax.broadcasted_iota(jnp.int32, (1, length), 1) < count_ref[0]
+    rake = jnp.full((1, length), rake_ref[0], jnp.float32)
+    turn_ref[0:1, :] = jnp.where(alive, jnp.cos(rake), 0.0)
+    turn_ref[1:2, :] = jnp.where(alive, jnp.sin(rake), 0.0)
+    earlier = lax.broadcasted_iota(jnp.int32, (length, length), 0) < lax.broadcasted_iota(
+        jnp.int32, (length, length), 1
+    )
+    earlier_ref[...] = earlier.astype(jnp.float32).astype(jnp.bfloat16)
+    for copy in copies:
+        copy.wait()
     owner_index = lax.broadcasted_iota(jnp.int32, (owners, length), 0)
     hot = ((owner_index == owner_ref[...]) & alive).astype(jnp.float32)
-    earlier = lax.broadcasted_iota(jnp.int32, (length, length), 0) < lax.broadcasted_iota(
-        jnp.int32, (length, length), 1
-    )
-    before = jnp.dot(
-        hot.astype(jnp.bfloat16), earlier.astype(jnp.bfloat16), preferred_element_type=jnp.float32
-    )
+    before = jnp.dot(hot.astype(jnp.bfloat16), earlier_ref[...], preferred_element_type=jnp.float32)
     rank = jnp.sum(hot * before, axis=0, keepdims=True).astype(jnp.int32)
     onset = onset_ref[...]
-    whole = onset >> (LANES.bit_length() - 1)
-    base = row_ref[...] * (4 * rows + 1) + (rows - 1) - whole
-    rake = jnp.full((1, length), rake_ref[0], jnp.float32)
-    weight = jnp.where(alive, slip_ref[...], 0.0)
+    base = row_ref[...] * (4 * rows + 1) + (rows - 1) - (onset >> (LANES.bit_length() - 1))
     fields = (
         base.astype(jnp.float32),
         (onset & (LANES - 1)).astype(jnp.float32),
-        jnp.cos(rake) * weight,
-        jnp.sin(rake) * weight,
+        turn_ref[0:1, :] * slip_ref[...],
+        turn_ref[1:2, :] * slip_ref[...],
     )
     place = lax.broadcasted_iota(jnp.int32, (len(fields) * capacity, length), 0)
     pieces = []
@@ -84,7 +80,6 @@
             preferred_element_type=jnp.float32,
         )
         total = term if part == 0 else total + term
-    out_ref[...] = jnp.zeros_like(out_ref)
     out_ref[:, 0 : total.shape[1]] = total
 
 
@@ -221,7 +216,11 @@
         in_specs=[SMEM] * 2 + [ANY] * 4,
         out_specs=VMEM,
         scratch_shapes=[pltpu.VMEM((1, length), array.dtype) for array in listed]
-        + [pltpu.SemaphoreType.DMA((4,))],
+        + [
+            pltpu.SemaphoreType.DMA((4,)),
+            pltpu.VMEM((2, length), jnp.float32),
+            pltpu.VMEM((length, length), jnp.bfloat16),
+        ],
         compiler_params=SMALL,
         name="route",
     )(point_count, rake_angle, *[in_hbm(array) for array in listed])

time: 28.5 us -> 28.5 us (level)
  no operation moved by 1% of the time
where the time goes in v6:
time: 28.5 us; the launch traced here: 28.3 us
  blocking collectives  9.48 us (33%)
  starting transfers between devices  7.4 us (26%)
  Pallas kernels  5.96 us (21%)
  waiting for transfers between devices  4.14 us (15%)
  between operations  1.33 us (5%)
    all_to_all x1, blocking collectives, local(): lax.all_to_all(partial, 'owner', split_axis=0, concat_axis=0, tiled=True)  9.48 us
    all_to_all x1, starting transfers between devices, local(): lax.all_to_all(table.reshape(owners, 1, LANES), 'owner', split_axis=0, co...  7.4 us
    all_to_all x1, waiting for transfers between devices, local(): lax.all_to_all(table.reshape(owners, 1, LANES), 'owner', split_axis=0, co...  4.14 us
    pallas_call x1, Pallas kernels, local(): pl.pallas_call(functools.partial(project_kernel, rows, group, chunk), out...  2.29 us
    pallas_call x1, Pallas kernels, local(): pl.pallas_call(functools.partial(route_kernel, capacity, rows), out_shape...  1.63 us
    pallas_call x1, Pallas kernels, local(): pl.pallas_call(functools.partial(gather_kernel, capacity, rows), out_shap...  1.29 us
    pallas_call x1, Pallas kernels, local(): pl.pallas_call(smooth_kernel, out_shape=jax.ShapeDtypeStruct((rows, LANES...  0.75 us
  transfers between devices with their start and end apart: 1, of which 1 were waited for; matrix products, arithmetic and copies ran while one was open for 0% of the time, Pallas kernels for 8%

profile of v6, /device:TPU:0, one launch (start us, length us, event | category | flops | bytes accessed | tf_op | source)
XLA Modules:
  0.0 28.3 jit_solution(5515553007532250317)
XLA Ops:
  1.3 1.6 %route.1 = f32[16,128]{1,0:T(8,128)} custom-call(s32[1]{0:T(128)S(6)} %copy.11.refs_0_, f32[1]{0:T(128)S(6)} %copy.12.refs_1_, s32[1,128]{1,0:T(1,128)} %bitcast.11, s32[1,128]{1,0:T(1,128)} %refs_3_.1, s32[1,128]{1,0:T(1,128)} %refs_4_.1, f32[1,128]{1,0:T(1,128)} %refs_5_.1), custom_call_target="tpu_custom_call" | custom-call | tf_op jit(solution)/shard_map/route/pallas_call | solution.py:213
  2.9 7.4 %all-to-all-start = ((f32[16,1,128]{2,1,0:T(1,128)}), f32[16,1,128]{2,1,0:T(1,128)S(1)}, u32[]{:S(2)}, u32[]{:S(2)}) async-start(f32[16,1,128]{2,1,0:T(1,128)} %bitcast.4), calls=%async_computation | async-start | bytes 16384 | tf_op jit(solution)/shard_map/all_to_all | solution.py:227
  10.3 2.3 %project.1 = (f32[4224,128]{1,0:T(8,128)S(1)}, f32[64,128]{1,0:T(8,128)S(1)}) custom-call(f32[6,2,128]{2,1,0:T(2,128)} %bitcast.10, f32[1,64]{1,0:T(1,128)} %rate_ref.1, bf16[6,128,1024]{2,1,0:T(8,128)(2,1)} %bitcast.9), custom_call_target="tpu_custom_call" | custom-call | tf_op jit(solution)/shard_map/project/pallas_call | solution.py:231
  12.6 4.1 %all-to-all-done = f32[16,1,128]{2,1,0:T(1,128)S(1)} async-done(((f32[16,1,128]{2,1,0:T(1,128)}), f32[16,1,128]{2,1,0:T(1,128)S(1)}, u32[]{:S(2)}, u32[]{:S(2)}) %all-to-all-start) | async-done | bytes 8224 | tf_op jit(solution)/shard_map/all_to_all | solution.py:227
  16.8 1.3 %gather.1 = f32[16,8,128]{2,1,0:T(8,128)S(1)} custom-call(f32[16,128]{1,0:T(8,128)S(1)} %bitcast.8, f32[4224,128]{1,0:T(8,128)S(1)} %get-tuple-element.8.trace_ref), custom_call_target="tpu_custom_call" | custom-call | tf_op jit(solution)/shard_map/gather/pallas_call | solution.py:255
  18.1 9.5 %all_to_all.10.part_ref = f32[16,8,128]{2,1,0:T(8,128)S(1)} all-to-all(f32[16,8,128]{2,1,0:T(8,128)S(1)} %gather.1), channel_id=1, replica_groups=mesh['site'=2,'owner'=16] {'owner'}, dimensions={0} | all-to-all | bytes 131072 | tf_op jit(solution)/shard_map/all_to_all | solution.py:269
  27.6 0.7 %smooth.1 = f32[8,128]{1,0:T(8,128)} custom-call(f32[64,128]{1,0:T(8,128)S(1)} %get-tuple-element.7.rates_ref, f32[16,8,128]{2,1,0:T(8,128)S(1)} %all_to_all.10.part_ref), custom_call_target="tpu_custom_call" | custom-call | tf_op jit(solution)/shard_map/smooth/pallas_call | solution.py:270
Async XLA Ops:
  2.9 13.8 %all-to-all-start = ((f32[16,1,128]{2,1,0:T(1,128)}), f32[16,1,128]{2,1,0:T(1,128)S(1)}, u32[]{:S(2)}, u32[]{:S(2)}) async-start(f32[16,1,128]{2,1,0:T(1,128)} %bitcast.4), calls=%async_computation | async-start | bytes 16384 | tf_op jit(solution)/shard_map/all_to_all | solution.py:227

commit v7 on v5

--- a/solution.py
+++ b/solution.py
@@ -151,22 +151,25 @@
         lax.fori_loop(number * (chunk // group), (number + 1) * (chunk // group), one, 0)
 
 
-def gather_kernel(capacity, rows, sent_ref, trace_ref, out_ref, word_here, word_ref, scale_ref, arrived):
-    scales = pltpu.make_async_copy(sent_ref, scale_ref, arrived.at[0])
-    scales.start()
+def gather_kernel(
+    capacity, rows, sent_ref, trace_ref, out_ref, word_here, word_ref, column_ref, scale_ref, arrived
+):
     word_here[...] = (sent_ref[...] + 0.5).astype(jnp.int32)
-    words = pltpu.make_async_copy(word_here, word_ref, arrived.at[1])
+    words = pltpu.make_async_copy(word_here, word_ref, arrived)
     words.start()
+    column_ref[...] = sent_ref[...].T
+    for number in range(out_ref.shape[0]):
+        column = column_ref[2 * capacity : 4 * capacity, number : number + 1]
+        scale_ref[number] = jnp.broadcast_to(column, (2 * capacity, LANES))
     left = LANES - 1 - lax.broadcasted_iota(jnp.int32, (rows, LANES), 1)
-    scales.wait()
     words.wait()
     for number in range(out_ref.shape[0]):
         total = [jnp.zeros((rows, LANES), jnp.float32)] * 2
         for slot in range(capacity):
             base = word_ref[number, slot]
             shift = word_ref[number, slot + capacity]
-            first = scale_ref[number, slot + 2 * capacity]
-            second = scale_ref[number, slot + 3 * capacity]
+            first = scale_ref[number, slot : slot + 1, :]
+            second = scale_ref[number, slot + capacity : slot + capacity + 1, :]
             stays = left >= shift
             one_kind = jnp.where(
                 stays, trace_ref[pl.ds(base + 1, rows), :], trace_ref[pl.ds(base, rows), :]
@@ -261,8 +264,9 @@
         scratch_shapes=[
             pltpu.VMEM((owners, LANES), jnp.int32),
             pltpu.SMEM((owners, LANES), jnp.int32),
-            pltpu.SMEM((owners, LANES), jnp.float32),
-            pltpu.SemaphoreType.DMA((2,)),
+            pltpu.VMEM((LANES, owners), jnp.float32),
+            pltpu.VMEM((owners, 2 * capacity, LANES), jnp.float32),
+            pltpu.SemaphoreType.DMA,
         ],
         compiler_params=SMALL,
         name="gather",

time: 28.5 us -> 28.5 us (level)
  no operation moved by 1% of the time
where the time goes in v7:
time: 28.5 us; the launch traced here: 28.3 us
  blocking collectives  9.48 us (33%)
  starting transfers between devices  7.4 us (26%)
  Pallas kernels  5.95 us (21%)
  waiting for transfers between devices  4.14 us (15%)
  between operations  1.33 us (5%)
    all_to_all x1, blocking collectives, local(): lax.all_to_all(partial, 'owner', split_axis=0, concat_axis=0, tiled=True)  9.48 us
    all_to_all x1, starting transfers between devices, local(): lax.all_to_all(table.reshape(owners, 1, LANES), 'owner', split_axis=0, co...  7.4 us
    all_to_all x1, waiting for transfers between devices, local(): lax.all_to_all(table.reshape(owners, 1, LANES), 'owner', split_axis=0, co...  4.14 us
    pallas_call x1, Pallas kernels, local(): pl.pallas_call(functools.partial(project_kernel, rows, group, chunk), out...  2.29 us
    pallas_call x1, Pallas kernels, local(): pl.pallas_call(functools.partial(route_kernel, capacity, rows), out_shape...  1.63 us
    pallas_call x1, Pallas kernels, local(): pl.pallas_call(functools.partial(gather_kernel, capacity, rows), out_shap...  1.28 us
    pallas_call x1, Pallas kernels, local(): pl.pallas_call(smooth_kernel, out_shape=jax.ShapeDtypeStruct((rows, LANES...  0.75 us
  transfers between devices with their start and end apart: 1, of which 1 were waited for; matrix products, arithmetic and copies ran while one was open for 0% of the time, Pallas kernels for 8%

profile of v7, /device:TPU:0, one launch (start us, length us, event | category | flops | bytes accessed | tf_op | source)
XLA Modules:
  0.0 28.3 jit_solution(6998136114701875823)
XLA Ops:
  1.3 1.6 %route.1 = f32[16,128]{1,0:T(8,128)} custom-call(s32[1]{0:T(128)S(6)} %copy.11.refs_0_, f32[1]{0:T(128)S(6)} %copy.12.refs_1_, s32[1,128]{1,0:T(1,128)} %bitcast.11, s32[1,128]{1,0:T(1,128)} %refs_3_.1, s32[1,128]{1,0:T(1,128)} %refs_4_.1, f32[1,128]{1,0:T(1,128)} %refs_5_.1), custom_call_target="tpu_custom_call" | custom-call | tf_op jit(solution)/shard_map/route/pallas_call | solution.py:221
  2.9 7.4 %all-to-all-start = ((f32[16,1,128]{2,1,0:T(1,128)}), f32[16,1,128]{2,1,0:T(1,128)S(1)}, u32[]{:S(2)}, u32[]{:S(2)}) async-start(f32[16,1,128]{2,1,0:T(1,128)} %bitcast.4), calls=%async_computation | async-start | bytes 16384 | tf_op jit(solution)/shard_map/all_to_all | solution.py:231
  10.3 2.3 %project.1 = (f32[4224,128]{1,0:T(8,128)S(1)}, f32[64,128]{1,0:T(8,128)S(1)}) custom-call(f32[6,2,128]{2,1,0:T(2,128)} %bitcast.10, f32[1,64]{1,0:T(1,128)} %rate_ref.1, bf16[6,128,1024]{2,1,0:T(8,128)(2,1)} %bitcast.9), custom_call_target="tpu_custom_call" | custom-call | tf_op jit(solution)/shard_map/project/pallas_call | solution.py:235
  12.6 4.1 %all-to-all-done = f32[16,1,128]{2,1,0:T(1,128)S(1)} async-done(((f32[16,1,128]{2,1,0:T(1,128)}), f32[16,1,128]{2,1,0:T(1,128)S(1)}, u32[]{:S(2)}, u32[]{:S(2)}) %all-to-all-start) | async-done | bytes 8224 | tf_op jit(solution)/shard_map/all_to_all | solution.py:231
  16.8 1.3 %gather.1 = f32[16,8,128]{2,1,0:T(8,128)S(1)} custom-call(f32[16,128]{1,0:T(8,128)S(1)} %bitcast.8, f32[4224,128]{1,0:T(8,128)S(1)} %get-tuple-element.8.trace_ref), custom_call_target="tpu_custom_call" | custom-call | tf_op jit(solution)/shard_map/gather/pallas_call | solution.py:259
  18.1 9.5 %all_to_all.10.part_ref = f32[16,8,128]{2,1,0:T(8,128)S(1)} all-to-all(f32[16,8,128]{2,1,0:T(8,128)S(1)} %gather.1), channel_id=1, replica_groups=mesh['site'=2,'owner'=16] {'owner'}, dimensions={0} | all-to-all | bytes 131072 | tf_op jit(solution)/shard_map/all_to_all | solution.py:274
  27.5 0.7 %smooth.1 = f32[8,128]{1,0:T(8,128)} custom-call(f32[64,128]{1,0:T(8,128)S(1)} %get-tuple-element.7.rates_ref, f32[16,8,128]{2,1,0:T(8,128)S(1)} %all_to_all.10.part_ref), custom_call_target="tpu_custom_call" | custom-call | tf_op jit(solution)/shard_map/smooth/pallas_call | solution.py:275
Async XLA Ops:
  2.9 13.8 %all-to-all-start = ((f32[16,1,128]{2,1,0:T(1,128)}), f32[16,1,128]{2,1,0:T(1,128)S(1)}, u32[]{:S(2)}, u32[]{:S(2)}) async-start(f32[16,1,128]{2,1,0:T(1,128)} %bitcast.4), calls=%async_computation | async-start | bytes 16384 | tf_op jit(solution)/shard_map/all_to_all | solution.py:231
